TPU v7x, 32 devices: a whole 2x2x4 slice. The times are simulated.
32 devices in a mesh: batch: 8 (over z, x), th: 2 (over y), tw: 2 (over core).
Axes of the slice: x: 2, y: 2, z: 4, core: 2. Of those that a mesh axis runs over, the one named last changes fastest.
Arguments:
- images: bfloat16 [64, 24, 24, 768], P('batch', 'th', 'tw'), may hold values from -6 to 6
- valid_slots: int32 [64], P('batch'), may hold values 0 or 1
- region_ids: int32 [24, 24], P('th', 'tw'), may hold values from 0 to 3
- relative_index: int32 [144, 144], replicated, may hold values from 0 to 528
- entry_weight: bfloat16 [768, 2304], P(('batch', 'th', 'tw')), may hold values from -0.21875 to 0.21875
- entry_bias: bfloat16 [1536], P(('batch', 'th', 'tw')), may hold values from -2 to 2
- exit_weight: bfloat16 [768, 768], P(('batch', 'th', 'tw')), may hold values from -1 to 1
- exit_bias: bfloat16 [768], P(('batch', 'th', 'tw')), may hold values from -2 to 2
- expand_weight: bfloat16 [768, 3072], P(('batch', 'th', 'tw')), may hold values from -0.21875 to 0.21875
- expand_bias: bfloat16 [3072], P(('batch', 'th', 'tw')), may hold values from -2 to 2
- reduce_weight: bfloat16 [3072, 768], P(('batch', 'th', 'tw')), may hold values from -0.109375 to 0.109375
- reduce_bias: bfloat16 [768], P(('batch', 'th', 'tw')), may hold values from -2 to 2
- first_gain: bfloat16 [768], P(('batch', 'th', 'tw')), may hold values from 0.099609375 to 1.8984375
- first_shift: bfloat16 [768], P(('batch', 'th', 'tw')), may hold values from -2 to 2
- second_gain: bfloat16 [768], P(('batch', 'th', 'tw')), may hold values from 0.099609375 to 1.8984375
- second_shift: bfloat16 [768], P(('batch', 'th', 'tw')), may hold values from -2 to 2
- bias_table: bfloat16 [529, 24], replicated, may hold values from -4 to 4
- cotangent: bfloat16 [64, 24, 24, 768], P('batch', 'th', 'tw'), may hold values from -6 to 6
Outputs:
- output: bfloat16 [64, 24, 24, 768], P('batch', 'th', 'tw')
- images_grad: bfloat16 [64, 24, 24, 768], P('batch', 'th', 'tw')
- entry_weight_grad: float32 [768, 2304], P(('batch', 'th', 'tw'))
- entry_bias_grad: float32 [1536], P(('batch', 'th', 'tw'))
- exit_weight_grad: float32 [768, 768], P(('batch', 'th', 'tw'))
- exit_bias_grad: float32 [768], P(('batch', 'th', 'tw'))
- expand_weight_grad: float32 [768, 3072], P(('batch', 'th', 'tw'))
- expand_bias_grad: float32 [3072], P(('batch', 'th', 'tw'))
- reduce_weight_grad: float32 [3072, 768], P(('batch', 'th', 'tw'))
- reduce_bias_grad: float32 [768], P(('batch', 'th', 'tw'))
- first_gain_grad: float32 [768], P(('batch', 'th', 'tw'))
- first_shift_grad: float32 [768], P(('batch', 'th', 'tw'))
- second_gain_grad: float32 [768], P(('batch', 'th', 'tw'))
- second_shift_grad: float32 [768], P(('batch', 'th', 'tw'))
- bias_table_grad: float32 [529, 24], replicated
All inputs are finite; a program needn't handle non-finite values. No bound on the sum of `valid_slots` on one device may be relied on, other than what follows from the above.
Results may differ from a plain program's by a relative error of at most 0.013.
Values may be sent and summed in bfloat16 or wider, within the bound.
No kernel may reach another device: no remote copies, remote signals or barrier semaphores. Data moves between devices by JAX's collectives and lax.ppermute only.
A program may use at most 320 MiB of HBM per device.

v0:
```python
import jax
import jax.numpy as jnp
from jax import lax
from jax.sharding import PartitionSpec as P

MB = 4


EPS = 1e-05
MASK_FILL = -100.0
HALF_ROOT = 0.7071067811865476
INV_ROOT_TAU = 0.3989422804014327


def shifted(value, axis, steps):
    count = lax.axis_size(axis)
    pairs = [(source, (source + steps) % count) for source in range(count)]
    return lax.ppermute(value, axis, pairs)


def product(left_side, right_side):
    return jnp.dot(left_side, right_side, preferred_element_type=jnp.float32)


def product_swap(left_side, right_side):
    return lax.dot_general(
        left_side, right_side, (((1,), (1,)), ((), ())), preferred_element_type=jnp.float32
    )


def product_outer(left_side, right_side):
    return lax.dot_general(
        left_side, right_side, (((0,), (0,)), ((), ())), preferred_element_type=jnp.float32
    )


def norm_forward(field, gain_vector, shift_vector):
    centred = field - jnp.mean(field, axis=-1, keepdims=True)
    inverse = lax.rsqrt(jnp.mean(centred * centred, axis=-1, keepdims=True) + EPS)
    normed = centred * inverse
    return (normed * gain_vector + shift_vector, normed, inverse)


def norm_backward(grad_rows, normed, inverse, gain_vector):
    scaled = grad_rows * gain_vector
    first_mean = jnp.mean(scaled, axis=-1, keepdims=True)
    second_mean = jnp.mean(scaled * normed, axis=-1, keepdims=True)
    grad_field = inverse * (scaled - first_mean - normed * second_mean)
    return (grad_field, jnp.sum(grad_rows * normed, axis=0), jnp.sum(grad_rows, axis=0))


def score_block(queries, keys_low, score_scale, score_bias):
    raw_scores = jnp.einsum(
        "nqhd,nkhd->nhqk", queries, keys_low, preferred_element_type=jnp.float32
    )
    return raw_scores * score_scale + score_bias[None]


def window_values(tile_block):
    half_side = tile_block.shape[1] // 2
    arrived = shifted(tile_block[:, :half_side], "th", -1)
    stacked = jnp.concatenate([tile_block[:, half_side:], arrived], axis=1)
    beside = shifted(stacked[:, :, :half_side], "tw", -1)
    return jnp.concatenate([stacked[:, :, half_side:], beside], axis=2)


def tile_values(window_block):
    half_side = window_block.shape[1] // 2
    arrived = shifted(window_block[:, :, half_side:], "tw", 1)
    stacked = jnp.concatenate([arrived, window_block[:, :, :half_side]], axis=2)
    above = shifted(stacked[:, half_side:], "th", 1)
    return jnp.concatenate([above, stacked[:, :half_side]], axis=1)


def window_grads(tile_block):
    half_side = tile_block.shape[1] // 2
    arrived = shifted(tile_block[:, :half_side], "th", -1)
    stacked = jnp.concatenate([tile_block[:, half_side:], arrived], axis=1)
    beside = shifted(stacked[:, :, :half_side], "tw", -1)
    return jnp.concatenate([stacked[:, :, half_side:], beside], axis=2)


def tile_grads(window_block):
    half_side = window_block.shape[1] // 2
    arrived = shifted(window_block[:, :, half_side:], "tw", 1)
    stacked = jnp.concatenate([arrived, window_block[:, :, :half_side]], axis=2)
    above = shifted(stacked[:, half_side:], "th", 1)
    return jnp.concatenate([above, stacked[:, :half_side]], axis=1)


def body(
    images,
    valid_slots,
    region_ids,
    relative_index,
    entry_weight,
    entry_bias,
    exit_weight,
    exit_bias,
    expand_weight,
    expand_bias,
    reduce_weight,
    reduce_bias,
    first_gain,
    first_shift,
    second_gain,
    second_shift,
    bias_table,
    cotangent,
):
    window_side = images.shape[1]
    window_area = window_side * window_side
    model_width = images.shape[3]
    head_count = bias_table.shape[1]
    head_size = model_width // head_count
    score_scale = head_size ** (-0.5)
    per_batch = images.shape[0] // MB
    devices = lax.axis_size("batch") * lax.axis_size("th") * lax.axis_size("tw")
    table_full = bias_table.astype(jnp.float32)
    region_flat = region_ids.reshape(window_area)
    mask_add = jnp.where(region_flat[:, None] == region_flat[None, :], 0.0, MASK_FILL).astype(
        jnp.float32
    )
    score_bias = jnp.take(table_full, relative_index, axis=0).transpose(2, 0, 1) + mask_add[None]
    totals = [
        jnp.zeros((member.shape[0] * devices,) + member.shape[1:], jnp.float32)
        for member in (
            entry_weight,
            entry_bias,
            exit_weight,
            exit_bias,
            expand_weight,
            expand_bias,
            reduce_weight,
            reduce_bias,
            first_gain,
            first_shift,
            second_gain,
            second_shift,
        )
    ]
    table_total = jnp.zeros((head_count, window_area, window_area), jnp.float32)
    results = []
    input_grads = []
    split_shape = (per_batch, window_area, head_count, head_size)
    tile_shape = (per_batch, window_side, window_side, model_width)
    for micro_batch in range(MB):
        current = (
            lax.all_gather(entry_weight, ("batch", "th", "tw"), axis=0, tiled=True),
            lax.all_gather(entry_bias, ("batch", "th", "tw"), axis=0, tiled=True),
            lax.all_gather(exit_weight, ("batch", "th", "tw"), axis=0, tiled=True),
            lax.all_gather(exit_bias, ("batch", "th", "tw"), axis=0, tiled=True),
            lax.all_gather(expand_weight, ("batch", "th", "tw"), axis=0, tiled=True),
            lax.all_gather(expand_bias, ("batch", "th", "tw"), axis=0, tiled=True),
            lax.all_gather(reduce_weight, ("batch", "th", "tw"), axis=0, tiled=True),
            lax.all_gather(reduce_bias, ("batch", "th", "tw"), axis=0, tiled=True),
            lax.all_gather(first_gain, ("batch", "th", "tw"), axis=0, tiled=True),
            lax.all_gather(first_shift, ("batch", "th", "tw"), axis=0, tiled=True),
            lax.all_gather(second_gain, ("batch", "th", "tw"), axis=0, tiled=True),
            lax.all_gather(second_shift, ("batch", "th", "tw"), axis=0, tiled=True),
        )
        (
            weight_entry,
            bias_entry,
            weight_exit,
            bias_exit,
            weight_expand,
            bias_expand,
            weight_reduce,
            bias_reduce,
            gain_first,
            shift_first,
            gain_second,
            shift_second,
        ) = current
        gain_first_full = gain_first.astype(jnp.float32)
        gain_second_full = gain_second.astype(jnp.float32)
        lower_slot = micro_batch * per_batch
        flat_in = (
            images[lower_slot : lower_slot + per_batch].astype(jnp.float32).reshape(-1, model_width)
        )
        keep_rows = jnp.repeat(
            valid_slots[lower_slot : lower_slot + per_batch].astype(jnp.float32), window_area
        )[:, None]
        normed_first, hat_first, inv_first = norm_forward(
            flat_in, gain_first_full, shift_first.astype(jnp.float32)
        )
        windows = window_values(normed_first.astype(jnp.bfloat16).reshape(tile_shape)).reshape(
            -1, model_width
        )
        full_bias = jnp.concatenate(
            [
                bias_entry[:model_width],
                jnp.zeros((model_width,), jnp.bfloat16),
                bias_entry[model_width:],
            ]
        ).astype(jnp.float32)
        triple = (product(windows, weight_entry) + full_bias).astype(jnp.bfloat16)
        queries = triple[:, :model_width].reshape(split_shape)
        keys_low = triple[:, model_width : 2 * model_width].reshape(split_shape)
        values_low = triple[:, 2 * model_width :].reshape(split_shape)
        scores = score_block(queries, keys_low, score_scale, score_bias)
        row_top = jnp.max(scores, axis=-1, keepdims=True)
        raised = jnp.exp(scores - row_top)
        exp_total = jnp.sum(raised, axis=-1, keepdims=True)
        chances = raised / exp_total
        log_total = row_top + jnp.log(exp_total)
        chances_low = chances.astype(jnp.bfloat16)
        attended = (
            jnp.einsum(
                "nhqk,nkhd->nqhd", chances_low, values_low, preferred_element_type=jnp.float32
            )
            .reshape(-1, model_width)
            .astype(jnp.bfloat16)
        )
        branch = (product(attended, weight_exit) + bias_exit.astype(jnp.float32)).astype(
            jnp.bfloat16
        )
        branch_tiles = tile_values(branch.reshape(tile_shape)).reshape(-1, model_width)
        middle = flat_in + branch_tiles.astype(jnp.float32)
        normed_second, hat_second, inv_second = norm_forward(
            middle, gain_second_full, shift_second.astype(jnp.float32)
        )
        second_low = normed_second.astype(jnp.bfloat16)
        hidden = product(second_low, weight_expand) + bias_expand.astype(jnp.float32)
        activated_low = jax.nn.gelu(hidden, approximate=False).astype(jnp.bfloat16)
        feed_out = product(activated_low, weight_reduce) + bias_reduce.astype(jnp.float32)
        results.append(((middle + feed_out) * keep_rows).astype(jnp.bfloat16).reshape(tile_shape))
        grad_out = (
            cotangent[lower_slot : lower_slot + per_batch]
            .astype(jnp.float32)
            .reshape(-1, model_width)
            * keep_rows
        )
        grad_feed = grad_out.astype(jnp.bfloat16)
        totals[6] += product_outer(activated_low, grad_feed)
        totals[7] += jnp.sum(grad_feed.astype(jnp.float32), axis=0)
        normal_cdf = 0.5 * (1.0 + lax.erf(hidden * HALF_ROOT))
        gelu_slope = normal_cdf + hidden * INV_ROOT_TAU * jnp.exp(-0.5 * hidden * hidden)
        grad_hidden = (product_swap(grad_feed, weight_reduce) * gelu_slope).astype(jnp.bfloat16)
        totals[4] += product_outer(second_low, grad_hidden)
        totals[5] += jnp.sum(grad_hidden.astype(jnp.float32), axis=0)
        grad_second, gain_part, shift_part = norm_backward(
            product_swap(grad_hidden, weight_expand), hat_second, inv_second, gain_second_full
        )
        totals[10] += gain_part
        totals[11] += shift_part
        grad_middle = grad_out + grad_second
        grad_branch = window_grads(grad_middle.astype(jnp.bfloat16).reshape(tile_shape)).reshape(
            -1, model_width
        )
        totals[2] += product_outer(attended, grad_branch)
        totals[3] += jnp.sum(grad_branch.astype(jnp.float32), axis=0)
        grad_attended = (
            product_swap(grad_branch, weight_exit).astype(jnp.bfloat16).reshape(split_shape)
        )
        scores_again = score_block(queries, keys_low, score_scale, score_bias)
        chances_again = jnp.exp(scores_again - log_total)
        again_low = chances_again.astype(jnp.bfloat16)
        grad_values = jnp.einsum(
            "nhqk,nqhd->nkhd", again_low, grad_attended, preferred_element_type=jnp.float32
        )
        grad_chances = jnp.einsum(
            "nqhd,nkhd->nhqk", grad_attended, values_low, preferred_element_type=jnp.float32
        )
        grad_scores = chances_again * (
            grad_chances - jnp.sum(chances_again * grad_chances, axis=-1, keepdims=True)
        )
        scores_low = grad_scores.astype(jnp.bfloat16)
        table_total = table_total + jnp.sum(scores_low.astype(jnp.float32), axis=0)
        grad_queries = (
            jnp.einsum("nhqk,nkhd->nqhd", scores_low, keys_low, preferred_element_type=jnp.float32)
            * score_scale
        )
        grad_keys = (
            jnp.einsum("nhqk,nqhd->nkhd", scores_low, queries, preferred_element_type=jnp.float32)
            * score_scale
        )
        grad_triple = jnp.concatenate(
            [
                grad_queries.reshape(-1, model_width),
                grad_keys.reshape(-1, model_width),
                grad_values.reshape(-1, model_width),
            ],
            axis=1,
        ).astype(jnp.bfloat16)
        totals[0] += product_outer(windows, grad_triple)
        column_sums = jnp.sum(grad_triple.astype(jnp.float32), axis=0)
        totals[1] += jnp.concatenate([column_sums[:model_width], column_sums[2 * model_width :]])
        grad_windows = product_swap(grad_triple, weight_entry).astype(jnp.bfloat16)
        grad_first = (
            tile_grads(grad_windows.reshape(tile_shape))
            .reshape(-1, model_width)
            .astype(jnp.float32)
        )
        grad_input, gain_part, shift_part = norm_backward(
            grad_first, hat_first, inv_first, gain_first_full
        )
        totals[8] += gain_part
        totals[9] += shift_part
        input_grads.append((grad_input + grad_middle).astype(jnp.bfloat16).reshape(tile_shape))
    shares = (
        lax.psum_scatter(totals[0], ("batch", "th", "tw"), scatter_dimension=0, tiled=True),
        lax.psum_scatter(totals[1], ("batch", "th", "tw"), scatter_dimension=0, tiled=True),
        lax.psum_scatter(totals[2], ("batch", "th", "tw"), scatter_dimension=0, tiled=True),
        lax.psum_scatter(totals[3], ("batch", "th", "tw"), scatter_dimension=0, tiled=True),
        lax.psum_scatter(totals[4], ("batch", "th", "tw"), scatter_dimension=0, tiled=True),
        lax.psum_scatter(totals[5], ("batch", "th", "tw"), scatter_dimension=0, tiled=True),
        lax.psum_scatter(totals[6], ("batch", "th", "tw"), scatter_dimension=0, tiled=True),
        lax.psum_scatter(totals[7], ("batch", "th", "tw"), scatter_dimension=0, tiled=True),
        lax.psum_scatter(totals[8], ("batch", "th", "tw"), scatter_dimension=0, tiled=True),
        lax.psum_scatter(totals[9], ("batch", "th", "tw"), scatter_dimension=0, tiled=True),
        lax.psum_scatter(totals[10], ("batch", "th", "tw"), scatter_dimension=0, tiled=True),
        lax.psum_scatter(totals[11], ("batch", "th", "tw"), scatter_dimension=0, tiled=True),
    )
    table_rows = jax.ops.segment_sum(
        table_total.transpose(1, 2, 0).reshape(-1, head_count),
        relative_index.reshape(-1),
        num_segments=bias_table.shape[0],
    )
    table_grad = lax.psum(table_rows, ("batch", "th", "tw"))
    return (
        jnp.concatenate(results, axis=0),
        jnp.concatenate(input_grads, axis=0),
        shares[0],
        shares[1],
        shares[2],
        shares[3],
        shares[4],
        shares[5],
        shares[6],
        shares[7],
        shares[8],
        shares[9],
        shares[10],
        shares[11],
        table_grad,
    )


def solution(mesh):
    in_specs = (
        P("batch", "th", "tw", None),
        P("batch"),
        P("th", "tw"),
        P(),
        P(("batch", "th", "tw"), None),
        P(("batch", "th", "tw")),
        P(("batch", "th", "tw"), None),
        P(("batch", "th", "tw")),
        P(("batch", "th", "tw"), None),
        P(("batch", "th", "tw")),
        P(("batch", "th", "tw"), None),
        P(("batch", "th", "tw")),
        P(("batch", "th", "tw")),
        P(("batch", "th", "tw")),
        P(("batch", "th", "tw")),
        P(("batch", "th", "tw")),
        P(),
        P("batch", "th", "tw", None),
    )
    out_specs = (
        P("batch", "th", "tw", None),
        P("batch", "th", "tw", None),
        P(("batch", "th", "tw"), None),
        P(("batch", "th", "tw")),
        P(("batch", "th", "tw"), None),
        P(("batch", "th", "tw")),
        P(("batch", "th", "tw"), None),
        P(("batch", "th", "tw")),
        P(("batch", "th", "tw"), None),
        P(("batch", "th", "tw")),
        P(("batch", "th", "tw")),
        P(("batch", "th", "tw")),
        P(("batch", "th", "tw")),
        P(("batch", "th", "tw")),
        P(),
    )
    return jax.shard_map(body, mesh=mesh, in_specs=in_specs, out_specs=out_specs, check_vma=False)
```

profile of v0, /device:TPU:0, one launch (start us, length us, event | category | flops | bytes accessed | tf_op | source)
XLA Modules:
  0.0 1508.7 jit_solution(5913347226648305999)
XLA Ops:
  16.2 43.0 %all-reduce.17 = (bf16[3072]{0:T(1024)(128)(2,1)}, bf16[768]{0:T(1024)(128)(2,1)S(1)}, bf16[768]{0:T(1024)(128)(2,1)S(1)}, bf16[1536]{0:T(1024)(128)(2,1)S(1)}, ...) all-reduce(bf16[3072]{0:T(1024)(128)(2,1)S(1)} %dynamic-update-slic, ...), channel_id=1, replica_groups=mesh['batch'=8,'th'=2,'tw'=2] {'batch','th','tw'}, use_global_device_ids=true, to_apply=%add.6 | all-reduce | flops 9216 | bytes 36864
  92.6 39.0 %gather_fusion = f32[20736,24]{1,0:T(8,128)} fusion(f32[529,24]{1,0:T(8,128)S(1)} %copy.415, s32[21504]{0:T(1024)S(1)} %pad_clamp_fusion), kind=kCustom, calls=%fused_computation | custom fusion | bytes 4064256 | tf_op jit(solution)/shard_map/jit(_take)/gather | solution.py:124
  131.6 12.6 copy.416
  404.6 12.5 fusion.21
  417.1 7.2 convert_reduce_fusion.6
  426.1 10.1 fusion.18
  436.2 5.7 convert_reduce_fusion.7
  445.8 10.0 fusion.24
  466.0 6.0 convert_reduce_fusion.4
  521.6 5.5 fusion.110
  550.0 5.5 fusion.104
  580.6 5.5 fusion.107
  696.9 10.2 copy.520
  707.2 113.8 %scatter_custom_fusion = f32[529,24]{1,0:T(8,128)} fusion(s32[20736]{0:T(1024)} %reshape.1048, f32[20736,24]{1,0:T(8,128)} %bitcast.197, f32[]{:T(128)} %constant.42.clone.1), kind=kCustom, calls=%fused_computation.461 | custom fusion | flops 497664 | bytes 51296 | tf_op jit(solution)/shard_map/scatter-add | solution.py:316
  839.7 6.3 collective-permute-done.27
  871.9 6.6 add_add_fusion.2
  894.7 11.0 add_add_fusion.1
  911.3 5.5 fusion.214
  922.1 16.1 %add_add_fusion = f32[3072,768]{1,0:T(8,128)} fusion(f32[3072,768]{1,0:T(8,128)} %fusion.214, f32[3072,768]{1,0:T(8,128)} %fusion.212, f32[3072,768]{1,0:T(8,128)S(1)} %fusion.213, f32[288,768]{1,0:T(8,128)S(1)} %copy-done.59, f32[288]{0:T(512)S(1)} %copy-done.213, f32[288,3072]{1,0:T(8,128)} %copy-done.229), kind=kOutput, calls=%fused_computation.2 | convolution fusion | flops 1423982592 | bytes 42173568 | tf_op jit(solution)/shard_map/dot_general | solution.py:32
  944.3 12.1 fusion.139
  1027.9 66.0 %reduce-scatter.7.cloned.1.call-done = f32[24,768]{1,0:T(8,128)} async-done(((f32[768,768]{1,0:T(8,128)}), f32[24,768]{1,0:T(8,128)}) %reduce-scatter.7.cloned.1.call-update) | async-done | bytes 73744 | tf_op jit(solution)/shard_map/reduce_scatter | solution.py:305
  1093.9 124.9 %reduce-scatter.5.cloned.1.call-done = f32[24,2304]{1,0:T(8,128)} async-done(((f32[768,2304]{1,0:T(8,128)}), f32[24,2304]{1,0:T(8,128)}) %reduce-scatter.5.cloned.1.call-update) | async-done | bytes 221200 | tf_op jit(solution)/shard_map/reduce_scatter | solution.py:303
  1218.8 141.6 %reduce-scatter.9.cloned.1.call-done = f32[24,3072]{1,0:T(8,128)} async-done(((f32[768,3072]{1,0:T(8,128)}), f32[24,3072]{1,0:T(8,128)}) %reduce-scatter.9.cloned.1.call-update) | async-done | bytes 294928 | tf_op jit(solution)/shard_map/reduce_scatter | solution.py:307
  1360.4 141.7 %reduce-scatter.11.cloned.1.call-done = f32[96,768]{1,0:T(8,128)} async-done(((f32[3072,768]{1,0:T(8,128)}), f32[96,768]{1,0:T(8,128)}) %reduce-scatter.11.cloned.1.call-update) | async-done | bytes 294928 | tf_op jit(solution)/shard_map/reduce_scatter | solution.py:309
  (981 shorter events, 673.2 us)
Async XLA Ops:
  7.2 193.8 %all-gather.5.cloned.1.call-start = ((), (), s32[]{:S(2)}) async-start(), calls=%async_computation.4 | async-start | bytes 3649536 | tf_op jit(solution)/shard_map/all_gather | solution.py:149
  7.9 287.9 %all-gather.7.cloned.1.call-start = ((), (), s32[]{:S(2)}) async-start(), calls=%async_computation.5 | async-start | bytes 1216512 | tf_op jit(solution)/shard_map/all_gather | solution.py:151
  8.7 395.9 %all-gather.9.cloned.1.call-start = ((), (), s32[]{:S(2)}) async-start(), calls=%async_computation.6 | async-start | bytes 4866048 | tf_op jit(solution)/shard_map/all_gather | solution.py:153
  9.4 407.7 %all-gather.11.cloned.1.call-start = ((), (), s32[]{:S(2)}) async-start(), calls=%async_computation.7 | async-start | bytes 4866048 | tf_op jit(solution)/shard_map/all_gather | solution.py:155
  68.5 109.1 %collective-permute-start = (bf16[2,6,12,768]{3,2,1,0:T(8,128)(2,1)}, bf16[2,6,12,768]{3,2,1,0:T(8,128)(2,1)}, u32[]{:S(2)}, u32[]{:S(2)}) collective-permute-start(bf16[2,6,12,768]{3,2,1,0:T(8,128)(2,1)} %get-tuple-element.193), channel_id=1, source_target_pairs={{0,2},{2,0},{1,3},{3,1},{4,6},{6,4},{5,7},{7,5},{8,10},{10,8},{9,1... | collective-permute-start | bytes 663560 | tf_op jit(solution)/shard_map/ppermute | solution.py:18
  72.1 106.9 %collective-permute-start.4 = (bf16[2,6,12,768]{3,2,1,0:T(8,128)(2,1)}, bf16[2,6,12,768]{3,2,1,0:T(8,128)(2,1)}, u32[]{:S(2)}, u32[]{:S(2)}) collective-permute-start(bf16[2,6,12,768]{3,2,1,0:T(8,128)(2,1)} %get-tuple-element.199), channel_id=1, source_target_pairs={{0,2},{2,0},{1,3},{3,1},{4,6},{6,4},{5,7},{7,5},{8,10},{10,8},{9,1... | collective-permute-start | bytes 663560 | tf_op jit(solution)/shard_map/ppermute | solution.py:18
  73.1 108.4 %collective-permute-start.8 = (bf16[2,6,12,768]{3,2,1,0:T(8,128)(2,1)}, bf16[2,6,12,768]{3,2,1,0:T(8,128)(2,1)}, u32[]{:S(2)}, u32[]{:S(2)}) collective-permute-start(bf16[2,6,12,768]{3,2,1,0:T(8,128)(2,1)} %get-tuple-element.205), channel_id=1, source_target_pairs={{0,2},{2,0},{1,3},{3,1},{4,6},{6,4},{5,7},{7,5},{8,10},{10,8},{9,1... | collective-permute-start | bytes 663560 | tf_op jit(solution)/shard_map/ppermute | solution.py:18
  76.1 107.6 %collective-permute-start.12 = (bf16[2,6,12,768]{3,2,1,0:T(8,128)(2,1)}, bf16[2,6,12,768]{3,2,1,0:T(8,128)(2,1)}, u32[]{:S(2)}, u32[]{:S(2)}) collective-permute-start(bf16[2,6,12,768]{3,2,1,0:T(8,128)(2,1)} %get-tuple-element.211), channel_id=1, source_target_pairs={{0,2},{2,0},{1,3},{3,1},{4,6},{6,4},{5,7},{7,5},{8,10},{10,8},{9,1... | collective-permute-start | bytes 663560 | tf_op jit(solution)/shard_map/ppermute | solution.py:18
  76.1 939.9 %all-reduce.20.cloned.1.call-start = ((), (), s32[]{:S(2)}) async-start(), calls=%async_computation.12 | async-start | bytes 638976
  302.5 52.2 %collective-permute-start.6 = (bf16[2,12,6,768]{3,2,1,0:T(8,128)(2,1)}, bf16[2,12,6,768]{3,2,1,0:T(8,128)(2,1)}, u32[]{:S(2)}, u32[]{:S(2)}) collective-permute-start(bf16[2,12,6,768]{3,2,1,0:T(8,128)(2,1)} %get-tuple-element.194), channel_id=1, source_target_pairs={{0,1},{1,0},{2,3},{3,2},{4,5},{5,4},{6,7},{7,6},{8,9},{9,8},{10,11... | collective-permute-start | bytes 663560 | tf_op jit(solution)/shard_map/ppermute | solution.py:18
  321.4 36.6 %collective-permute-start.10 = (bf16[2,12,6,768]{3,2,1,0:T(8,128)(2,1)}, bf16[2,12,6,768]{3,2,1,0:T(8,128)(2,1)}, u32[]{:S(2)}, u32[]{:S(2)}) collective-permute-start(bf16[2,12,6,768]{3,2,1,0:T(8,128)(2,1)} %get-tuple-element.200), channel_id=1, source_target_pairs={{0,1},{1,0},{2,3},{3,2},{4,5},{5,4},{6,7},{7,6},{8,9},{9,8},{10,11... | collective-permute-start | bytes 663560 | tf_op jit(solution)/shard_map/ppermute | solution.py:18
  364.4 28.6 %collective-permute-start.3 = (bf16[2,6,12,768]{3,2,1,0:T(8,128)(2,1)}, bf16[2,6,12,768]{3,2,1,0:T(8,128)(2,1)S(1)}, u32[]{:S(2)}, u32[]{:S(2)}) collective-permute-start(bf16[2,6,12,768]{3,2,1,0:T(8,128)(2,1)} %fusion.206), channel_id=1, source_target_pairs={{0,2},{2,0},{1,3},{3,1},{4,6},{6,4},{5,7},{7,5},{8,10},{10,8},{9,1... | collective-permute-start | bytes 663560 | tf_op jit(solution)/shard_map/ppermute | solution.py:18
  501.4 97.4 %collective-permute-start.17 = (bf16[2,12,6,768]{3,2,1,0:T(8,128)(2,1)}, bf16[2,12,6,768]{3,2,1,0:T(8,128)(2,1)}, u32[]{:S(2)}, u32[]{:S(2)}) collective-permute-start(bf16[2,12,6,768]{3,2,1,0:T(8,128)(2,1)} %get-tuple-element.167), channel_id=1, source_target_pairs={{0,1},{1,0},{2,3},{3,2},{4,5},{5,4},{6,7},{7,6},{8,9},{9,8},{10,11... | collective-permute-start | bytes 663560 | tf_op jit(solution)/shard_map/ppermute | solution.py:18
  506.5 61.8 %collective-permute-start.25 = (bf16[2,12,6,768]{3,2,1,0:T(8,128)(2,1)}, bf16[2,12,6,768]{3,2,1,0:T(8,128)(2,1)}, u32[]{:S(2)}, u32[]{:S(2)}) collective-permute-start(bf16[2,12,6,768]{3,2,1,0:T(8,128)(2,1)} %get-tuple-element.179), channel_id=1, source_target_pairs={{0,1},{1,0},{2,3},{3,2},{4,5},{5,4},{6,7},{7,6},{8,9},{9,8},{10,11... | collective-permute-start | bytes 663560 | tf_op jit(solution)/shard_map/ppermute | solution.py:18
  509.8 28.1 %collective-permute-start.29 = (bf16[2,12,6,768]{3,2,1,0:T(8,128)(2,1)}, bf16[2,12,6,768]{3,2,1,0:T(8,128)(2,1)}, u32[]{:S(2)}, u32[]{:S(2)}) collective-permute-start(bf16[2,12,6,768]{3,2,1,0:T(8,128)(2,1)} %get-tuple-element.185), channel_id=1, source_target_pairs={{0,1},{1,0},{2,3},{3,2},{4,5},{5,4},{6,7},{7,6},{8,9},{9,8},{10,11... | collective-permute-start | bytes 663560 | tf_op jit(solution)/shard_map/ppermute | solution.py:18
  657.4 164.9 %collective-permute-start.22 = (bf16[2,12,6,768]{3,2,1,0:T(8,128)(2,1)}, bf16[2,12,6,768]{3,2,1,0:T(8,128)(2,1)}, u32[]{:S(2)}, u32[]{:S(2)}) collective-permute-start(bf16[2,12,6,768]{3,2,1,0:T(8,128)(2,1)} %get-tuple-element.170), channel_id=1, source_target_pairs={{0,1},{1,0},{2,3},{3,2},{4,5},{5,4},{6,7},{7,6},{8,9},{9,8},{10,11... | collective-permute-start | bytes 663560 | tf_op jit(solution)/shard_map/ppermute | solution.py:18
  668.5 156.5 %collective-permute-start.30 = (bf16[2,12,6,768]{3,2,1,0:T(8,128)(2,1)}, bf16[2,12,6,768]{3,2,1,0:T(8,128)(2,1)}, u32[]{:S(2)}, u32[]{:S(2)}) collective-permute-start(bf16[2,12,6,768]{3,2,1,0:T(8,128)(2,1)} %get-tuple-element.182), channel_id=1, source_target_pairs={{0,1},{1,0},{2,3},{3,2},{4,5},{5,4},{6,7},{7,6},{8,9},{9,8},{10,11... | collective-permute-start | bytes 663560 | tf_op jit(solution)/shard_map/ppermute | solution.py:18
  677.4 149.3 %collective-permute-start.26 = (bf16[2,12,6,768]{3,2,1,0:T(8,128)(2,1)}, bf16[2,12,6,768]{3,2,1,0:T(8,128)(2,1)}, u32[]{:S(2)}, u32[]{:S(2)}) collective-permute-start(bf16[2,12,6,768]{3,2,1,0:T(8,128)(2,1)} %get-tuple-element.176), channel_id=1, source_target_pairs={{0,1},{1,0},{2,3},{3,2},{4,5},{5,4},{6,7},{7,6},{8,9},{9,8},{10,11... | collective-permute-start | bytes 663560 | tf_op jit(solution)/shard_map/ppermute | solution.py:18
  686.6 142.7 %collective-permute-start.18 = (bf16[2,12,6,768]{3,2,1,0:T(8,128)(2,1)}, bf16[2,12,6,768]{3,2,1,0:T(8,128)(2,1)}, u32[]{:S(2)}, u32[]{:S(2)}) collective-permute-start(bf16[2,12,6,768]{3,2,1,0:T(8,128)(2,1)} %get-tuple-element.164), channel_id=1, source_target_pairs={{0,1},{1,0},{2,3},{3,2},{4,5},{5,4},{6,7},{7,6},{8,9},{9,8},{10,11... | collective-permute-start | bytes 663560 | tf_op jit(solution)/shard_map/ppermute | solution.py:18
  830.4 21.1 %collective-permute-start.19 = (bf16[2,6,12,768]{3,2,1,0:T(8,128)(2,1)S(1)}, bf16[2,6,12,768]{3,2,1,0:T(8,128)(2,1)S(1)}, u32[]{:S(2)}, u32[]{:S(2)}) collective-permute-start(bf16[2,6,12,768]{3,2,1,0:T(8,128)(2,1)S(1)} %fusion.198), channel_id=1, source_target_pairs={{0,2},{2,0},{1,3},{3,1},{4,6},{6,4},{5,7},{7,5},{8,10},{10,8},{9,1... | collective-permute-start | bytes 663560 | tf_op jit(solution)/shard_map/ppermute | solution.py:18
  857.8 236.1 %reduce-scatter.7.cloned.1.call-start = ((), (), s32[]{:S(2)}) async-start(), calls=%async_computation.9 | async-start | bytes 2433024 | tf_op jit(solution)/shard_map/reduce_scatter | solution.py:305
  863.2 355.6 %reduce-scatter.5.cloned.1.call-start = ((), (), s32[]{:S(2)}) async-start(), calls=%async_computation.8 | async-start | bytes 7299072 | tf_op jit(solution)/shard_map/reduce_scatter | solution.py:303
  878.5 481.9 %reduce-scatter.9.cloned.1.call-start = ((), (), s32[]{:S(2)}) async-start(), calls=%async_computation.10 | async-start | bytes 9732096 | tf_op jit(solution)/shard_map/reduce_scatter | solution.py:307
  905.7 596.3 %reduce-scatter.11.cloned.1.call-start = ((), (), s32[]{:S(2)}) async-start(), calls=%async_computation.11 | async-start | bytes 9732096 | tf_op jit(solution)/shard_map/reduce_scatter | solution.py:309
  (257 other events, 4823.1 us)
Sparse Core Ops, SparseCore 0:
  10.9 62.7 all-gather.4
  76.6 52.7 all-gather.6
  132.4 62.4 all-gather.8
  197.7 61.8 all-gather.10
  857.9 129.4 all-reduce.19
  993.1 100.7 reduce-scatter.6
  1100.1 118.5 reduce-scatter.4
  1225.2 135.0 reduce-scatter.8
  1366.8 135.1 reduce-scatter.10
where the time goes:
time: 1520 us; the launch traced here: 1510 us
  waiting for transfers between devices  506 us (33%)
  local copies, waits for them, and re-layouts  369 us (24%)
  matrix products  280 us (18%)
  other arithmetic  272 us (18%)
  blocking collectives  43 us (3%)
  starting transfers between devices  22.2 us (1%)
  between operations  17 us (1%)
    reduce_scatter x1, waiting for transfers between devices, body(): lax.psum_scatter(totals[6], ('batch', 'th', 'tw'), scatter_dimension=0, t...  142 us
    reduce_scatter x1, waiting for transfers between devices, body(): lax.psum_scatter(totals[4], ('batch', 'th', 'tw'), scatter_dimension=0, t...  142 us
    reduce_scatter x1, waiting for transfers between devices, body(): lax.psum_scatter(totals[0], ('batch', 'th', 'tw'), scatter_dimension=0, t...  125 us
    scatter-add x1, other arithmetic, body(): jax.ops.segment_sum(table_total.transpose(1, 2, 0).reshape(-1, head_count...  114 us
    dot_general x16, matrix products, product(): return jnp.dot(left_side, right_side, preferred_element_type=jnp.float32)  84.5 us
    dot_general x16, matrix products, product_outer(): lax.dot_general(left_side, right_side, (((0,), (0,)), ((), ())), preferre...  83.5 us
    reduce_scatter x1, waiting for transfers between devices, body(): lax.psum_scatter(totals[2], ('batch', 'th', 'tw'), scatter_dimension=0, t...  66 us
    dot_general x16, matrix products, product_swap(): lax.dot_general(left_side, right_side, (((1,), (1,)), ((), ())), preferre...  52.9 us
  transfers between devices with their start and end apart: 41, of which 13 were waited for; matrix products, arithmetic and copies ran while one was open for 52% of the time, Pallas kernels for 0%

commit v1 on v0

v1 whole, which is shorter than its diff:
```python
import functools

import jax
import jax.numpy as jnp
from jax import lax
from jax.experimental import pallas as pl
from jax.experimental.pallas import tpu as pltpu
from jax.sharding import PartitionSpec as P

EPS = 1e-05
MASK_FILL = -100.0
HALF_ROOT = 0.7071067811865476
INV_ROOT_TAU = 0.3989422804014327
BF = jnp.bfloat16
F32 = jnp.float32
VMEM_BYTES = 60 << 20


def dot_nn(a, b):
    return lax.dot_general(a, b, (((1,), (0,)), ((), ())), preferred_element_type=F32)


def dot_nt(a, b):
    return lax.dot_general(a, b, (((1,), (1,)), ((), ())), preferred_element_type=F32)


def dot_tn(a, b):
    return lax.dot_general(a, b, (((0,), (0,)), ((), ())), preferred_element_type=F32)


def swap(value, axis, mask):
    count = lax.axis_size(axis)
    return lax.ppermute(value, axis, [(i, i ^ mask) for i in range(count)])


def pick(value, index):
    return lax.dynamic_index_in_dim(value, index, 0, keepdims=False)


def params(**kw):
    return pltpu.CompilerParams(vmem_limit_bytes=VMEM_BYTES, **kw)


def cost(flops, nbytes, trans=0):
    return pl.CostEstimate(flops=int(flops), bytes_accessed=int(nbytes), transcendentals=int(trans))


def place_kernel(widths, rows, fold, order_ref, mine_ref, theirs_ref, *outs):
    core = order_ref[order_ref.shape[0] - 1]
    own = mine_ref[0]
    other = theirs_ref[0]
    first = jnp.where(core == 0, own, other)
    second = jnp.where(core == 0, other, own)
    at = 0
    for out, width, parts in zip(outs, widths, fold):
        for part in range(parts):
            out[part * rows : (part + 1) * rows, :] = first[:, at : at + width]
            out[(parts + part) * rows : (parts + part + 1) * rows, :] = second[:, at : at + width]
            at += width


def gather_blocks(block, widths, fold, y_first):
    rows = block.shape[0]
    batch, high, core = (lax.axis_index(a) for a in ("batch", "th", "tw"))
    held = jnp.stack([block] + [swap(block, "batch", m << 1) for m in (1, 2, 3)])
    steps = [("th", 1), ("batch", 1)] if y_first else [("batch", 1), ("th", 1)]
    for axis, mask in steps:
        held = jnp.concatenate([held, swap(held, axis, mask)])
    theirs = swap(held, "tw", 1)
    chips = held.shape[0]
    target = jnp.arange(chips, dtype=jnp.int32) ^ (batch * 2 + high).astype(jnp.int32)
    y_bit, x_bit, z_bits = target & 1, (target >> 1) & 1, target >> 2
    low, top = (y_bit, x_bit) if y_first else (x_bit, y_bit)
    order = jnp.concatenate([top * 8 + low * 4 + z_bits, core.astype(jnp.int32)[None]])
    shapes = [(chips * 2 * rows * f, w) for w, f in zip(widths, fold)]
    return pl.pallas_call(
        functools.partial(place_kernel, widths, rows, fold),
        grid_spec=pltpu.PrefetchScalarGridSpec(
            num_scalar_prefetch=1,
            grid=(chips,),
            in_specs=[pl.BlockSpec((1,) + block.shape, lambda c, o: (o[c], 0, 0))] * 2,
            out_specs=[pl.BlockSpec((2 * rows * f, w), lambda c, o: (c, 0)) for w, f in zip(widths, fold)],
        ),
        out_shape=[jax.ShapeDtypeStruct(s, block.dtype) for s in shapes],
        compiler_params=params(),
        cost_estimate=cost(0, 4 * chips * block.size * 2),
        name="place",
    )(order, held, theirs)


def scatter_sum(whole, rows, y_first):
    batch, high, core = (lax.axis_index(a) for a in ("batch", "th", "tw"))
    width = whole.shape[1]
    kept = whole.reshape(-1, 2, rows, width).swapaxes(0, 1)
    got = swap(pick(kept, 1 - core), "tw", 1)
    kept = pick(kept, core).astype(F32) + got.astype(F32)
    kept = kept.reshape(-1, 2, 2, rows, width)
    kept = kept.transpose(2, 1, 0, 3, 4)
    if not y_first:
        kept = kept.swapaxes(0, 1)
    x_bit = batch & 1
    plan = [("th", high), ("batch", x_bit)] if y_first else [("batch", x_bit), ("th", high)]
    for axis, bit in plan:
        got = swap(pick(kept, 1 - bit).astype(BF), axis, 1)
        kept = pick(kept, bit) + got.astype(F32)
    spot = batch >> 1
    total = pick(kept, spot)
    for mask in (1, 2, 3):
        total = total + swap(pick(kept, spot ^ mask).astype(BF), "batch", mask << 1).astype(F32)
    return total


def sum_everywhere(value):
    value = value + swap(value, "tw", 1)
    value = value + swap(value, "th", 1)
    step = 1
    while step < lax.axis_size("batch"):
        value = value + swap(value, "batch", step)
        step *= 2
    return value


def tiles_to_images(tiles):
    high, core = lax.axis_index("th"), lax.axis_index("tw")
    side, width = tiles.shape[1], tiles.shape[3]
    half = side // 2
    split = tiles.reshape((2, 2, -1) + tiles.shape[1:])
    own = pick(split, high)
    got = swap(pick(split, 1 - high), "th", 1)
    rows = jnp.where(high == 0, jnp.stack([own, got]), jnp.stack([got, own]))
    rows = rows.swapaxes(0, 1)
    own = pick(rows, core)
    got = swap(pick(rows, 1 - core), "tw", 1)
    grid = jnp.where(core == 0, jnp.stack([own, got]), jnp.stack([got, own]))
    grid = grid.transpose(2, 1, 3, 0, 4, 5).reshape(-1, 2 * side, 2 * side, width)
    grid = jnp.roll(grid, (-half, -half), axis=(1, 2))
    return grid.reshape(-1, 2, side, 2, side, width).transpose(0, 1, 3, 2, 4, 5)


def images_to_tiles(windows):
    high, core = lax.axis_index("th"), lax.axis_index("tw")
    count, side, width = windows.shape[0], windows.shape[3], windows.shape[5]
    half = side // 2
    grid = windows.transpose(0, 1, 3, 2, 4, 5).reshape(count, 2 * side, 2 * side, width)
    grid = jnp.roll(grid, (half, half), axis=(1, 2))
    grid = grid.reshape(count, 2, side, 2, side, width).transpose(3, 1, 0, 2, 4, 5)
    own = pick(grid, core)
    got = swap(pick(grid, 1 - core), "tw", 1)
    rows = jnp.where(core == 0, jnp.stack([own, got]), jnp.stack([got, own]))
    rows = rows.swapaxes(0, 1)
    own = pick(rows, high)
    got = swap(pick(rows, 1 - high), "th", 1)
    tiles = jnp.where(high == 0, jnp.stack([own, got]), jnp.stack([got, own]))
    return tiles.reshape((-1, side, side, width))


def look_kernel(index_ref, table_ref, out_ref):
    entries = table_ref.shape[1]
    for k in range(index_ref.shape[0]):
        spots = index_ref[k : k + 1, :]
        level = lax.broadcasted_iota(jnp.int32, (entries, spots.shape[1]), 0)
        hot = jnp.where(level == spots, 1.0, 0.0).astype(BF)
        out_ref[k] = dot_nn(table_ref[...], hot)


def look_up(table_t, index_t, step):
    area = index_t.shape[0]
    heads, entries = table_t.shape
    return pl.pallas_call(
        look_kernel,
        grid=(area // step,),
        in_specs=[
            pl.BlockSpec((step, area), lambda i: (i, 0)),
            pl.BlockSpec((heads, entries), lambda i: (0, 0)),
        ],
        out_specs=pl.BlockSpec((step, heads, area), lambda i: (i, 0, 0)),
        out_shape=jax.ShapeDtypeStruct((area, heads, area), F32),
        compiler_params=params(),
        cost_estimate=cost(2 * 256 * entries * area * area, area * area * heads * 4),
        name="look",
    )(index_t, table_t)


def count_kernel(index_ref, grad_ref, out_ref):
    @pl.when(pl.program_id(0) == 0)
    def _():
        out_ref[...] = jnp.zeros_like(out_ref)

    entries = out_ref.shape[0]
    total = jnp.zeros(out_ref.shape, F32)
    for k in range(index_ref.shape[0]):
        spots = index_ref[k : k + 1, :]
        level = lax.broadcasted_iota(jnp.int32, (entries, spots.shape[1]), 0)
        hot = jnp.where(level == spots, 1.0, 0.0).astype(BF)
        total = total + dot_nt(hot, grad_ref[k])
    out_ref[...] += total


def count_up(grads, index_t, entries, step):
    area, columns, _ = grads.shape
    return pl.pallas_call(
        count_kernel,
        grid=(area // step,),
        in_specs=[
            pl.BlockSpec((step, area), lambda i: (i, 0)),
            pl.BlockSpec((step, columns, area), lambda i: (i, 0, 0)),
        ],
        out_specs=pl.BlockSpec((entries, columns), lambda i: (0, 0)),
        out_shape=jax.ShapeDtypeStruct((entries, columns), F32),
        compiler_params=params(),
        cost_estimate=cost(2 * 256 * entries * area * area, grads.size * 2),
        name="count",
    )(index_t, grads)


def lanes_of(shape, head, size):
    lane = lax.broadcasted_iota(jnp.int32, shape, 1)
    return (lane >= head * size) & (lane < (head + 1) * size)


def attend_kernel(width, size, triple_ref, bias_ref, mask_ref, out_ref, lse_ref):
    scale = size ** (-0.5)
    per = 128 // size
    area = triple_ref.shape[1]
    wall = mask_ref[0]

    def group(g, carry):
        at = pl.multiple_of(g * 128, 128)
        queries = triple_ref[0, :, pl.ds(at, 128)]
        keys = triple_ref[0, :, pl.ds(pl.multiple_of(width + at, 128), 128)]
        values = triple_ref[0, :, pl.ds(pl.multiple_of(2 * width + at, 128), 128)]
        values_t = values.astype(F32).T.astype(BF)
        found = []
        for i in range(per):
            own = lanes_of((area, 128), i, size)
            head = g * per + i
            scores = dot_nt(jnp.where(own, keys, jnp.zeros_like(keys)), queries) * scale
            scores = scores + (bias_ref[head] + wall)
            top = jnp.max(scores, axis=0, keepdims=True)
            raised = jnp.exp(scores - top)
            total = jnp.sum(raised, axis=0, keepdims=True)
            chances = (raised * (1.0 / total)).astype(BF)
            lse_ref[0, pl.ds(head, 1), :] = top + jnp.log(total)
            found.append(dot_nn(values_t[i * size : (i + 1) * size, :], chances))
        out_ref[0, :, pl.ds(at, 128)] = jnp.concatenate(found, axis=0).T.astype(BF)
        return carry

    lax.fori_loop(0, width // 128, group, 0)


def attend(triple, bias, masks, size):
    count, area, wide = triple.shape
    width = wide // 3
    heads = bias.shape[0]
    per_image = masks.shape[0]
    return pl.pallas_call(
        functools.partial(attend_kernel, width, size),
        grid=(count,),
        in_specs=[
            pl.BlockSpec((1, area, wide), lambda i: (i, 0, 0)),
            pl.BlockSpec((heads, area, area), lambda i: (0, 0, 0)),
            pl.BlockSpec((1, area, area), lambda i: (i % per_image, 0, 0)),
        ],
        out_specs=[
            pl.BlockSpec((1, area, width), lambda i: (i, 0, 0)),
            pl.BlockSpec((1, heads, area), lambda i: (i, 0, 0)),
        ],
        out_shape=[
            jax.ShapeDtypeStruct((count, area, width), BF),
            jax.ShapeDtypeStruct((count, heads, area), F32),
        ],
        compiler_params=params(),
        cost_estimate=cost(count * heads * area * area * 4 * 256, triple.size * 3, count * heads * area * area),
        name="attend",
    )(triple, bias, masks)


def attend_back_kernel(width, size, triple_ref, given_ref, bias_ref, mask_ref, lse_ref, out_ref, total_ref):
    scale = size ** (-0.5)
    per = 128 // size
    area = triple_ref.shape[1]
    wall = mask_ref[0]

    @pl.when(pl.program_id(0) == 0)
    def _():
        total_ref[...] = jnp.zeros_like(total_ref)

    def group(g, carry):
        at = pl.multiple_of(g * 128, 128)
        queries = triple_ref[0, :, pl.ds(at, 128)]
        keys = triple_ref[0, :, pl.ds(pl.multiple_of(width + at, 128), 128)]
        values = triple_ref[0, :, pl.ds(pl.multiple_of(2 * width + at, 128), 128)]
        given = given_ref[0, :, pl.ds(at, 128)]
        keys_t = keys.astype(F32).T.astype(BF)
        zero = jnp.zeros_like(keys)
        to_queries = []
        to_keys = jnp.zeros((area, 128), F32)
        to_values = jnp.zeros((area, 128), F32)
        for i in range(per):
            own = lanes_of((area, 128), i, size)
            head = g * per + i
            scores = dot_nt(jnp.where(own, keys, zero), queries) * scale
            scores = scores + (bias_ref[head] + wall)
            chances = jnp.exp(scores - lse_ref[0, pl.ds(head, 1), :])
            to_values = to_values + dot_nn(chances.astype(BF), jnp.where(own, given, zero))
            slopes = dot_nt(jnp.where(own, values, zero), given)
            scaled = chances * slopes
            delta = jnp.sum(scaled, axis=0, keepdims=True)
            moved = (scaled - chances * delta).astype(BF)
            total_ref[head] += moved.astype(F32)
            to_keys = to_keys + dot_nn(moved, jnp.where(own, queries, zero))
            to_queries.append(dot_nn(keys_t[i * size : (i + 1) * size, :], moved))
        out_ref[0, :, pl.ds(at, 128)] = (jnp.concatenate(to_queries, axis=0).T * scale).astype(BF)
        out_ref[0, :, pl.ds(pl.multiple_of(width + at, 128), 128)] = (to_keys * scale).astype(BF)
        out_ref[0, :, pl.ds(pl.multiple_of(2 * width + at, 128), 128)] = to_values.astype(BF)
        return carry

    lax.fori_loop(0, width // 128, group, 0)


def attend_back(triple, given, bias, masks, lse, size):
    count, area, wide = triple.shape
    width = wide // 3
    heads = bias.shape[0]
    per_image = masks.shape[0]
    return pl.pallas_call(
        functools.partial(attend_back_kernel, width, size),
        grid=(count,),
        in_specs=[
            pl.BlockSpec((1, area, wide), lambda i: (i, 0, 0)),
            pl.BlockSpec((1, area, width), lambda i: (i, 0, 0)),
            pl.BlockSpec((heads, area, area), lambda i: (0, 0, 0)),
            pl.BlockSpec((1, area, area), lambda i: (i % per_image, 0, 0)),
            pl.BlockSpec((1, heads, area), lambda i: (i, 0, 0)),
        ],
        out_specs=[
            pl.BlockSpec((1, area, wide), lambda i: (i, 0, 0)),
            pl.BlockSpec((heads, area, area), lambda i: (0, 0, 0)),
        ],
        out_shape=[
            jax.ShapeDtypeStruct((count, area, wide), BF),
            jax.ShapeDtypeStruct((heads, area, area), F32),
        ],
        compiler_params=params(),
        cost_estimate=cost(count * heads * area * area * 10 * 256, triple.size * 6, count * heads * area * area),
        name="attend_back",
    )(triple, given, bias, masks, lse)


def feed_kernel(tile, second_ref, given_ref, up_ref, up_bias_ref, down_ref,
                out_ref, back_ref, up_grad_ref, down_grad_ref, bias_grad_ref, active_ref, moved_ref):
    first = pl.program_id(0) == 0

    @pl.when(first)
    def _():
        out_ref[...] = jnp.zeros_like(out_ref)
        back_ref[...] = jnp.zeros_like(back_ref)

    bias_grad_ref[...] = jnp.zeros_like(bias_grad_ref)

    def part(r, carry):
        rows = pl.ds(pl.multiple_of(r * tile, tile), tile)
        hidden = dot_nn(second_ref[rows, :], up_ref[...]) + up_bias_ref[...]
        chance = 0.5 * (1.0 + lax.erf(hidden * HALF_ROOT))
        active = (hidden * chance).astype(BF)
        slope = chance + hidden * INV_ROOT_TAU * jnp.exp(-0.5 * hidden * hidden)
        moved = (dot_nt(given_ref[rows, :], down_ref[...]) * slope).astype(BF)
        active_ref[rows, :] = active
        moved_ref[rows, :] = moved
        bias_grad_ref[...] += jnp.sum(moved.astype(F32), axis=0, keepdims=True)
        out_ref[rows, :] += dot_nn(active, down_ref[...])
        back_ref[rows, :] += dot_nt(moved, up_ref[...])
        return carry

    lax.fori_loop(0, second_ref.shape[0] // tile, part, 0)
    down_grad_ref[...] = dot_tn(active_ref[...], given_ref[...]).astype(BF)
    up_grad_ref[...] = dot_tn(second_ref[...], moved_ref[...]).astype(BF)


def feed(second, given, up, up_bias, down, chunk=512, tile=288):
    tokens, width = second.shape
    hidden = up.shape[1]
    fixed = pl.BlockSpec((tokens, width), lambda j: (0, 0), pipeline_mode=pl.Buffered(1))
    return pl.pallas_call(
        functools.partial(feed_kernel, tile),
        grid=(hidden // chunk,),
        in_specs=[
            fixed,
            fixed,
            pl.BlockSpec((width, chunk), lambda j: (0, j)),
            pl.BlockSpec((1, chunk), lambda j: (0, j)),
            pl.BlockSpec((chunk, width), lambda j: (j, 0)),
        ],
        out_specs=[
            pl.BlockSpec((tokens, width), lambda j: (0, 0)),
            pl.BlockSpec((tokens, width), lambda j: (0, 0)),
            pl.BlockSpec((width, chunk), lambda j: (0, j)),
            pl.BlockSpec((chunk, width), lambda j: (j, 0)),
            pl.BlockSpec((1, chunk), lambda j: (0, j)),
        ],
        out_shape=[
            jax.ShapeDtypeStruct((tokens, width), F32),
            jax.ShapeDtypeStruct((tokens, width), F32),
            jax.ShapeDtypeStruct((width, hidden), BF),
            jax.ShapeDtypeStruct((hidden, width), BF),
            jax.ShapeDtypeStruct((1, hidden), F32),
        ],
        scratch_shapes=[pltpu.VMEM((tokens, chunk), BF), pltpu.VMEM((tokens, chunk), BF)],
        compiler_params=params(),
        cost_estimate=cost(12 * tokens * width * hidden, 16 * width * hidden, 2 * tokens * hidden),
        name="feed",
    )(second, given, up, up_bias, down)


def norm_forward(field, gain_vector, shift_vector):
    centred = field - jnp.mean(field, axis=-1, keepdims=True)
    inverse = lax.rsqrt(jnp.mean(centred * centred, axis=-1, keepdims=True) + EPS)
    normed = centred * inverse
    return (normed * gain_vector + shift_vector, normed, inverse)


def norm_backward(grad_rows, normed, inverse, gain_vector):
    scaled = grad_rows * gain_vector
    first_mean = jnp.mean(scaled, axis=-1, keepdims=True)
    second_mean = jnp.mean(scaled * normed, axis=-1, keepdims=True)
    grad_field = inverse * (scaled - first_mean - normed * second_mean)
    return (grad_field, jnp.sum(grad_rows * normed, axis=0), jnp.sum(grad_rows, axis=0))


def body(
    images,
    valid_slots,
    region_ids,
    relative_index,
    entry_weight,
    entry_bias,
    exit_weight,
    exit_bias,
    expand_weight,
    expand_bias,
    reduce_weight,
    reduce_bias,
    first_gain,
    first_shift,
    second_gain,
    second_shift,
    bias_table,
    cotangent,
):
    every = ("batch", "th", "tw")
    side, width = images.shape[1], images.shape[3]
    area = side * side
    heads = bias_table.shape[1]
    size = width // heads
    rows = entry_weight.shape[0]
    devices = lax.axis_size("batch") * lax.axis_size("th") * lax.axis_size("tw")
    fan = reduce_weight.shape[0] // rows
    paired = rows % 8 == 0 and lax.axis_size("batch") == 8
    high, core, spot = lax.axis_index("th"), lax.axis_index("tw"), lax.axis_index("batch")
    owner = high * 2 + core

    smalls = (entry_bias, exit_bias, expand_bias, reduce_bias, first_gain, first_shift, second_gain, second_shift)
    small_cols = [s.shape[0] // rows for s in smalls]
    packed = jnp.concatenate([s.reshape(rows, -1) for s in smalls], axis=1)
    packed = jnp.pad(packed, ((0, 0), (0, 128 - packed.shape[1])))
    if paired:
        weight_entry, packed_full = gather_blocks(
            jnp.concatenate([entry_weight, packed], axis=1), (entry_weight.shape[1], 128), (1, 1), False
        )
    else:
        weight_entry = lax.all_gather(entry_weight, every, axis=0, tiled=True)
        packed_full = lax.all_gather(packed, every, axis=0, tiled=True)
    vectors = []
    at = 0
    for columns in small_cols:
        vectors.append(packed_full[:, at : at + columns].reshape(-1).astype(F32))
        at += columns
    (bias_entry, bias_exit, bias_expand, bias_reduce, gain_first, shift_first, gain_second, shift_second) = vectors

    image_windows = tiles_to_images(images)
    shape = image_windows.shape
    count = shape[0] * 4
    flat_low = image_windows.reshape(-1, width)

    if paired:
        reduce_cols = jnp.concatenate([reduce_weight[i * rows : (i + 1) * rows] for i in range(fan)], axis=1)
        weight_exit, weight_expand, weight_reduce = gather_blocks(
            jnp.concatenate([exit_weight, expand_weight, reduce_cols], axis=1),
            (width, expand_weight.shape[1], width),
            (1, 1, fan),
            True,
        )
    else:
        weight_exit = lax.all_gather(exit_weight, every, axis=0, tiled=True)
        weight_expand = lax.all_gather(expand_weight, every, axis=0, tiled=True)
        weight_reduce = lax.all_gather(reduce_weight, every, axis=0, tiled=True)
    given_windows = tiles_to_images(cotangent)

    entries = -(-bias_table.shape[0] // 128) * 128
    table_t = jnp.pad(bias_table, ((0, entries - bias_table.shape[0]), (0, 0))).T
    index_t = relative_index.T
    bias = look_up(table_t, index_t, 8).swapaxes(0, 1)
    region_flat = region_ids.reshape(1, area)
    region_rows = jnp.concatenate([region_flat, swap(region_flat, "tw", 1)])
    region_rows = jnp.where(core == 0, region_rows, region_rows[::-1])[None]
    region_all = jnp.concatenate([region_rows, swap(region_rows, "th", 1)])
    region_all = jnp.where(high == 0, region_all, region_all[::-1]).reshape(4, area)
    masks = jnp.where(region_all[:, :, None] == region_all[:, None, :], 0.0, MASK_FILL).astype(F32)

    flat_in = flat_low.astype(F32)
    normed_first, hat_first, inv_first = norm_forward(flat_in, gain_first, shift_first)
    windows = normed_first.astype(BF)
    full_bias = jnp.concatenate([bias_entry[:width], jnp.zeros((width,), F32), bias_entry[width:]])
    triple = (dot_nn(windows, weight_entry) + full_bias).astype(BF).reshape(count, area, 3 * width)
    attended, lse = attend(triple, bias, masks, size)
    attended = attended.reshape(-1, width)
    branch = (dot_nn(attended, weight_exit) + bias_exit).astype(BF)
    middle = flat_in + branch.astype(F32)
    normed_second, hat_second, inv_second = norm_forward(middle, gain_second, shift_second)
    second_low = normed_second.astype(BF)
    keep = lax.dynamic_slice_in_dim(valid_slots, owner * shape[0], shape[0]).astype(F32)
    keep_rows = jnp.repeat(keep, 4 * area)[:, None]
    grad_out = given_windows.reshape(-1, width).astype(F32) * keep_rows
    grad_feed = grad_out.astype(BF)
    feed_out, grad_second, up_grad, down_grad, up_bias_grad = feed(
        second_low, grad_feed, weight_expand, bias_expand[None], weight_reduce
    )
    result = ((middle + feed_out + bias_reduce) * keep_rows).astype(BF)
    output = images_to_tiles(result.reshape(shape))

    grad_middle, second_gain_part, second_shift_part = norm_backward(grad_second, hat_second, inv_second, gain_second)
    grad_middle = grad_out + grad_middle
    grad_branch = grad_middle.astype(BF)
    exit_grad = dot_tn(attended, grad_branch).astype(BF)
    grad_attended = dot_nt(grad_branch, weight_exit).astype(BF).reshape(count, area, width)
    grad_triple, moved_total = attend_back(triple, grad_attended, bias, masks, lse, size)
    grad_triple = grad_triple.reshape(-1, 3 * width)
    entry_grad = dot_tn(windows, grad_triple).astype(BF)
    grad_first = dot_nt(grad_triple, weight_entry).astype(BF).astype(F32)
    grad_input, first_gain_part, first_shift_part = norm_backward(grad_first, hat_first, inv_first, gain_first)
    images_grad = images_to_tiles((grad_input + grad_middle).astype(BF).reshape(shape))

    spread = moved_total.swapaxes(0, 1)
    spread_high = spread.astype(BF)
    spread_low = (spread - spread_high.astype(F32)).astype(BF)
    table_part = count_up(jnp.concatenate([spread_high, spread_low], axis=1), index_t, entries, 8)
    table_part = table_part[: bias_table.shape[0], :heads] + table_part[: bias_table.shape[0], heads:]

    column_sums = jnp.sum(grad_triple.astype(F32), axis=0)
    small_parts = [
        column_sums[:width],
        column_sums[2 * width :],
        jnp.sum(grad_branch.astype(F32), axis=0),
        up_bias_grad[0],
        jnp.sum(grad_feed.astype(F32), axis=0),
        first_gain_part,
        first_shift_part,
        second_gain_part,
        second_shift_part,
    ]
    lane = 128
    flat_parts = jnp.concatenate(small_parts + [table_part.reshape(-1)])
    length = flat_parts.shape[0]
    padded = -(-length // (8 * lane)) * 8 * lane
    summed = sum_everywhere(jnp.pad(flat_parts, (0, padded - length)).reshape(-1, lane)).reshape(-1)
    here = (spot * 2 + high) * 2 + core
    small_outs = []
    at = 0
    for small in smalls:
        part = small.shape[0]
        small_outs.append(lax.dynamic_slice_in_dim(summed, at + here * part, part))
        at += part * devices
    (entry_bias_out, exit_bias_out, expand_bias_out, reduce_bias_out, *norm_outs) = small_outs
    table_grad = summed[at : at + bias_table.size].reshape(bias_table.shape)

    if paired:
        down_out = scatter_sum(down_grad, rows * fan, True)
        up_out = scatter_sum(up_grad, rows, False)
        exit_out = scatter_sum(exit_grad, rows, True)
        entry_out = scatter_sum(entry_grad, rows, False)
    else:
        entry_out, exit_out, up_out, down_out = (
            lax.psum_scatter(g.astype(F32), every, scatter_dimension=0, tiled=True)
            for g in (entry_grad, exit_grad, up_grad, down_grad)
        )
    return (
        output,
        images_grad,
        entry_out,
        entry_bias_out,
        exit_out,
        exit_bias_out,
        up_out,
        expand_bias_out,
        down_out,
        reduce_bias_out,
        *norm_outs,
        table_grad,
    )


def solution(mesh):
    every = ("batch", "th", "tw")
    tiles = P("batch", "th", "tw", None)
    matrix, vector = P(every, None), P(every)
    in_specs = (tiles, P("batch"), P("th", "tw"), P()) + (matrix, vector) * 4 + (vector,) * 4 + (P(), tiles)
    out_specs = (tiles, tiles) + (matrix, vector) * 4 + (vector,) * 4 + (P(),)
    return jax.shard_map(body, mesh=mesh, in_specs=in_specs, out_specs=out_specs, check_vma=False)
```

time: 1520 us -> 779 us (0.51)
  waiting for transfers between devices: 506 us -> 202 us
  matrix products: 280 us -> 31.9 us
  local copies, waits for them, and re-layouts: 369 us -> 145 us
  Pallas kernels: 0 us -> 216 us
  other arithmetic: 272 us -> 115 us
  blocking collectives: 43 us -> 0 us
  starting transfers between devices: 22.2 us -> 53.5 us
    reduce_scatter x4 -> x0, waiting for transfers between devices: 474 us -> none  [the longest x1 142 us: body(): lax.psum_scatter(totals[6], ('batch', 'th', 'tw'), scatter_dimension=0, t...]
    dot_general x72 -> x6, matrix products: 280 us -> 31.9 us  [the longest x2 13.3 us: dot_nn(): lax.dot_general(a, b, (((1,), (0,)), ((), ())), preferred_element_type=F32)]
    pallas_call x0 -> x7, Pallas kernels: none -> 216 us  [the longest x1 62.5 us: attend_back(): pl.pallas_call(functools.partial(attend_back_kernel, width, size), grid=(...]
    ppermute x32 -> x51, waiting for transfers between devices: 29.2 us -> 202 us  [swap(): return lax.ppermute(value, axis, [(i, i ^ mask) for i in range(count)])]
    reshape x65 -> x16, local copies, waits for them, and re-layouts: 140 us -> 16.8 us  [the longest x8 6.13 us: body(): packed = jnp.concatenate([s.reshape(rows, -1) for s in smalls], axis=1)]
    scatter-add x1 -> x0, other arithmetic: 114 us -> none  [body(): jax.ops.segment_sum(table_total.transpose(1, 2, 0).reshape(-1, head_count...]
    slice x39 -> x12, local copies, waits for them, and re-layouts: 59.5 us -> 7.44 us  [the longest x4 3.5 us: images_to_tiles(): grid = jnp.roll(grid, (half, half), axis=(1, 2))]
    gather x2 -> x0, local copies, waits for them, and re-layouts: 51.6 us -> none  [body(): jnp.take(table_full, relative_index, axis=0).transpose(2, 0, 1)]
  transfers between devices with their start and end apart: 41 -> 51, of which waited for: 13 -> 22; matrix products, arithmetic and copies ran while one was open for 52% -> 29% of each run, Pallas kernels for 0% -> 12%
where the time goes in v1:
time: 779 us; the launch traced here: 765 us
  Pallas kernels  216 us (28%)
  waiting for transfers between devices  202 us (26%)
  local copies, waits for them, and re-layouts  145 us (19%)
  other arithmetic  115 us (15%)
  starting transfers between devices  53.5 us (7%)
  matrix products  31.9 us (4%)
    ppermute x51, waiting for transfers between devices, swap(): return lax.ppermute(value, axis, [(i, i ^ mask) for i in range(count)])  202 us
    pallas_call x1, Pallas kernels, attend_back(): pl.pallas_call(functools.partial(attend_back_kernel, width, size), grid=(...  62.5 us
    ppermute x51, starting transfers between devices, swap(): return lax.ppermute(value, axis, [(i, i ^ mask) for i in range(count)])  53.5 us
    pallas_call x1, Pallas kernels, attend(): pl.pallas_call(functools.partial(attend_kernel, width, size), grid=(count...  51.7 us
    pallas_call x1, Pallas kernels, feed(): pl.pallas_call(functools.partial(feed_kernel, tile), grid=(hidden // chun...  46.6 us
    pallas_call x2, Pallas kernels, gather_blocks(): pl.pallas_call(functools.partial(place_kernel, widths, rows, fold), grid_...  24.5 us
    unnamed x113, local copies, waits for them, and re-layouts  22.2 us
    dynamic_slice x10, local copies, waits for them, and re-layouts, pick(): return lax.dynamic_index_in_dim(value, index, 0, keepdims=False)  19.4 us
  transfers between devices with their start and end apart: 51, of which 22 were waited for; matrix products, arithmetic and copies ran while one was open for 29% of the time, Pallas kernels for 12%

profile of v1, /device:TPU:0, one launch (start us, length us, event | category | flops | bytes accessed | tf_op | source)
XLA Modules:
  0.0 765.4 jit_solution(2414585249761101162)
XLA Ops:
  43.5 13.1 %look.1 = f32[144,24,144]{2,1,0:T(8,128)} custom-call(s32[144,144]{1,0:T(8,128)} %bitcast.351, bf16[24,640]{1,0:T(8,128)(2,1)} %pad_bitcast_fusion.1.table_ref), custom_call_target="tpu_custom_call" | custom-call | flops 6794772480 | bytes 1990656 | tf_op jit(solution)/shard_map/look/pallas_call | solution.py:169
  94.7 19.0 %collective-permute-done.16 = bf16[2,2,12,12,768]{4,1,3,2,0:T(2,128)(2,1)S(1)} collective-permute-done((bf16[2,2,12,12,768]{4,1,3,2,0:T(2,128)(2,1)}, bf16[2,2,12,12,768]{4,1,3,2,0:T(2,128)(2,1)S(1)}, u32[]{:S(2)}, u32[]{:S(2)}) %collective-permute-start.16) | collective-permute-done | bytes 884768 | tf_op jit(solution)/shard_map/ppermute | solution.py:33
  120.6 40.2 %collective-permute-done.6 = bf16[8,24,2432]{2,1,0:T(8,128)(2,1)S(1)} collective-permute-done((bf16[8,24,2432]{2,1,0:T(8,128)(2,1)S(1)}, bf16[8,24,2432]{2,1,0:T(8,128)(2,1)S(1)}, u32[]{:S(2)}, u32[]{:S(2)}) %collective-permute-start.6) | collective-permute-done | bytes 933920 | tf_op jit(solution)/shard_map/ppermute | solution.py:33
  188.9 34.1 %collective-permute-done.14 = bf16[8,24,6912]{2,1,0:T(8,128)(2,1)S(1)} collective-permute-done((bf16[8,24,6912]{2,1,0:T(8,128)(2,1)S(1)}, bf16[8,24,6912]{2,1,0:T(8,128)(2,1)S(1)}, u32[]{:S(2)}, u32[]{:S(2)}) %collective-permute-start.14) | collective-permute-done | bytes 2654240 | tf_op jit(solution)/shard_map/ppermute | solution.py:33
  235.4 4.8 reshape.413
  251.9 4.8 reshape.407
  263.2 10.8 %place.2 = (bf16[768,2304]{1,0:T(8,128)(2,1)}, bf16[768,128]{1,0:T(8,128)(2,1)}) custom-call(s32[17]{0:T(128)} %pad_add_fusion.2.order_ref, bf16[16,24,2432]{2,1,0:T(8,128)(2,1)} %constant_dynamic-update-slice_fusion.5.mine_ref, bf16[16,24,2432]{2,1,0:T(8,128)(2,1)} %collective-permute-done.7.theirs_ref), custom_call_target="tpu_custom_call" | custom-call | bytes 7471104 | tf_op jit(solution)/shard_map/place/pallas_call | solution.py:76
  289.4 8.7 %fusion = bf16[1152,2304]{1,0:T(8,128)(2,1)} fusion(bf16[768,2304]{1,0:T(8,128)(2,1)} %get-tuple-element.30, f32[2304]{0:T(1024)S(1)} %pad_maximum_fusion.9, f32[1152,768]{1,0:T(8,128)S(1)} %copy-done.3, f32[768]{0:T(1024)} %copy-done.32, f32[768]{0:T(1024)S(1)} %get-tuple-element.86, f32[1152]{0:T(1024)} %rsqrt.21, f32[1152]{0:T(1024)} %div.27), kind=kOutput, calls=%fused_computation.1 | convolution fusion | flops 4086595584 | bytes 12410880 | tf_op jit(solution)/shard_map/dot_general | solution.py:20
  298.1 51.7 %attend.1 = (bf16[8,144,768]{2,1,0:T(8,128)(2,1)}, f32[8,24,144]{2,1,0:T(8,128)}) custom-call(bf16[8,144,2304]{2,1,0:T(8,128)(2,1)} %bitcast.360, f32[24,144,144]{2,1,0:T(8,128)} %bitcast.337, f32[4,144,144]{2,1,0:T(8,128)} %compare_select_fusion.mask_ref), custom_call_target="tpu_custom_call" | custom-call | flops 4076863488 | bytes 7962624 | tf_op jit(solution)/shard_map/attend/pallas_call | solution.py:256
  349.9 13.6 %place.3 = (bf16[768,768]{1,0:T(8,128)(2,1)}, bf16[768,3072]{1,0:T(8,128)(2,1)}, bf16[3072,768]{1,0:T(8,128)(2,1)}) custom-call(s32[17]{0:T(128)} %pad_add_fusion.3.order_ref, bf16[16,24,6912]{2,1,0:T(8,128)(2,1)} %constant_dynamic-update-slice_fusion.22.mine_ref, bf16[16,24,6912]{2,1,0:T(8,128)(2,1)} %collective-permute-done.15.theirs_ref), custom_call_target="tpu_custom_call" | custom-call | bytes 21233664 | tf_op jit(solution)/shard_map/place/pallas_call | solution.py:76
  370.6 46.6 %feed.1 = (f32[1152,768]{1,0:T(8,128)}, f32[1152,768]{1,0:T(8,128)}, bf16[768,3072]{1,0:T(8,128)(2,1)}, bf16[3072,768]{1,0:T(8,128)(2,1)}, f32[1,3072]{1,0:T(1,128)}) custom-call(bf16[1152,768]{1,0:T(8,128)(2,1)} %add_convert_fusion.1.second_ref, bf16[1152,768]{1,0:T(8,128)(2,1)} %multiply_convert_fusion.1.given_ref, ...), custom_call_target="tpu_custom_call" | custom-call | flops 32614907904 | bytes 37748736 | tf_op jit(solution)/shard_map/feed/pallas_call | solution.py:384
  421.4 5.4 convert_reduce_fusion.3
  432.5 62.5 %attend_back.1 = (bf16[8,144,2304]{2,1,0:T(8,128)(2,1)}, f32[24,144,144]{2,1,0:T(8,128)}) custom-call(bf16[8,144,2304]{2,1,0:T(8,128)(2,1)} %bitcast.361, bf16[8,144,768]{2,1,0:T(8,128)(2,1)} %bitcast.364, f32[24,144,144]{2,1,0:T(8,128)} %bitcast.338, f32[4,144,144]{2,1,0:T(8,128)} %compare_select_fusion.mask_ref, f32[8,24,144]{2,1,0:T(8,128)} %get-tuple-element.37.lse_ref), custom_call_target="tpu_custom_call" | custom-call | flops 10192158720 | bytes 15925248 | tf_op jit(solution)/shard_map/attend_back/pallas_call | solution.py:326
  498.6 7.7 %fusion.10 = (f32[768]{0:T(1024)S(1)}, f32[1152]{0:T(1024)S(1)}, f32[1152]{0:T(1024)S(1)}, f32[768]{0:T(1024)S(1)}, bf16[1152,768]{1,0:T(8,128)(2,1)S(1)}) fusion(f32[1152,768]{1,0:T(8,128)S(1)} %copy-done.4, f32[1152]{0:T(1024)S(1)} %copy-done.27, f32[1152]{0:T(1024)S(1)} %copy-done.26, f32[768]{0:T(1024)S(1)} %get-tuple-element.86, ...), kind=kOutput, calls=%fused_computation.21 | convolution fusion | flops 4086591744 | bytes 14183424 | tf_op jit(solution)/shard_map/dot_general | solution.py:24
  533.6 5.2 convolution_convert_fusion
  545.2 17.7 %count.1 = f32[640,48]{1,0:T(8,128)} custom-call(s32[144,144]{1,0:T(8,128)} %bitcast.352, bf16[144,48,144]{2,1,0:T(8,128)(2,1)} %pad_maximum_fusion.grad_ref), custom_call_target="tpu_custom_call" | custom-call | flops 6794772480 | bytes 1990656 | tf_op jit(solution)/shard_map/count/pallas_call | solution.py:201
  593.5 5.5 collective-permute-done.34
  606.2 5.2 broadcast_select_fusion.1
  626.1 16.0 %collective-permute-done.21 = bf16[2,2,12,12,768]{4,1,3,2,0:T(2,128)(2,1)S(1)} collective-permute-done((bf16[2,2,12,12,768]{4,1,3,2,0:T(2,128)(2,1)S(1)}, bf16[2,2,12,12,768]{4,1,3,2,0:T(2,128)(2,1)S(1)}, u32[]{:S(2)}, u32[]{:S(2)}) %collective-permute-start.21) | collective-permute-done | bytes 884768 | tf_op jit(solution)/shard_map/ppermute | solution.py:33
  644.7 14.4 %collective-permute-done.19 = bf16[2,2,12,12,768]{4,1,3,2,0:T(2,128)(2,1)S(1)} collective-permute-done((bf16[2,2,12,12,768]{4,1,3,2,0:T(2,128)(2,1)S(1)}, bf16[2,2,12,12,768]{4,1,3,2,0:T(2,128)(2,1)S(1)}, u32[]{:S(2)}, u32[]{:S(2)}) %collective-permute-start.19) | collective-permute-done | bytes 884768 | tf_op jit(solution)/shard_map/ppermute | solution.py:33
  665.5 4.9 select_n.207
  674.5 5.0 select_n.204
  690.4 27.9 %collective-permute-done.24 = bf16[4,24,2304]{2,1,0:T(8,128)(2,1)S(1)} collective-permute-done((bf16[4,24,2304]{2,1,0:T(8,128)(2,1)S(1)}, bf16[4,24,2304]{2,1,0:T(8,128)(2,1)S(1)}, u32[]{:S(2)}, u32[]{:S(2)}) %collective-permute-start.24) | collective-permute-done | bytes 442400 | tf_op jit(solution)/shard_map/ppermute | solution.py:33
  749.6 10.1 %collective-permute-done.49 = bf16[96,768]{1,0:T(8,128)(2,1)S(1)} collective-permute-done((bf16[96,768]{1,0:T(8,128)(2,1)S(1)}, bf16[96,768]{1,0:T(8,128)(2,1)S(1)}, u32[]{:S(2)}, u32[]{:S(2)}) %collective-permute-start.49) | collective-permute-done | bytes 147488 | tf_op jit(solution)/shard_map/ppermute | solution.py:33
  (374 shorter events, 328.2 us)
Async XLA Ops:
  8.5 63.4 %collective-permute-start.3 = (bf16[24,2432]{1,0:T(8,128)(2,1)}, bf16[24,2432]{1,0:T(8,128)(2,1)}, u32[]{:S(2)}, u32[]{:S(2)}) collective-permute-start(bf16[24,2432]{1,0:T(8,128)(2,1)} %get-tuple-element.141), channel_id=1, source_target_pairs={{0,16},{4,20},{8,24},{12,28},{16,0},{20,4},{24,8},{28,12},{1,17},{... | collective-permute-start | bytes 350216 | tf_op jit(solution)/shard_map/ppermute | solution.py:33
  12.6 56.9 %collective-permute-start.2 = (bf16[24,2432]{1,0:T(8,128)(2,1)}, bf16[24,2432]{1,0:T(8,128)(2,1)}, u32[]{:S(2)}, u32[]{:S(2)}) collective-permute-start(bf16[24,2432]{1,0:T(8,128)(2,1)} %get-tuple-element.141), channel_id=1, source_target_pairs={{0,8},{4,12},{8,0},{12,4},{16,24},{20,28},{24,16},{28,20},{1,9},{5... | collective-permute-start | bytes 350216 | tf_op jit(solution)/shard_map/ppermute | solution.py:33
  14.2 59.9 %collective-permute-start.4 = (bf16[24,2432]{1,0:T(8,128)(2,1)}, bf16[24,2432]{1,0:T(8,128)(2,1)}, u32[]{:S(2)}, u32[]{:S(2)}) collective-permute-start(bf16[24,2432]{1,0:T(8,128)(2,1)} %get-tuple-element.141), channel_id=1, source_target_pairs={{0,24},{4,28},{8,16},{12,20},{16,8},{20,12},{24,0},{28,4},{1,25},{... | collective-permute-start | bytes 350216 | tf_op jit(solution)/shard_map/ppermute | solution.py:33
  15.0 41.6 %collective-permute-start.8 = (s32[1,144]{1,0:T(1,128)S(1)}, s32[1,144]{1,0:T(1,128)S(1)}, u32[]{:S(2)}, u32[]{:S(2)}) collective-permute-start(s32[1,144]{1,0:T(1,128)S(1)} %reshape.383), channel_id=1, source_target_pairs={{0,1},{1,0},{2,3},{3,2},{4,5},{5,4},{6,7},{7,6},{8,9},{9,8},{10,11... | collective-permute-start | bytes 1736 | tf_op jit(solution)/shard_map/ppermute | solution.py:33
  23.6 54.8 %collective-permute-start.12 = (bf16[24,6912]{1,0:T(8,128)(2,1)}, bf16[24,6912]{1,0:T(8,128)(2,1)}, u32[]{:S(2)}, u32[]{:S(2)}) collective-permute-start(bf16[24,6912]{1,0:T(8,128)(2,1)} %constant_dynamic-update-slice_fusion.11), channel_id=1, source_target_pairs={{0,24},{4,28},{8,16},{12,20},{16,8},{20,12},{24,0},{28,4},{1,25},{... | collective-permute-start | bytes 995336 | tf_op jit(solution)/shard_map/ppermute | solution.py:33
  74.1 39.6 %collective-permute-start.16 = (bf16[2,2,12,12,768]{4,1,3,2,0:T(2,128)(2,1)}, bf16[2,2,12,12,768]{4,1,3,2,0:T(2,128)(2,1)S(1)}, u32[]{:S(2)}, u32[]{:S(2)}) collective-permute-start(bf16[2,2,12,12,768]{4,1,3,2,0:T(2,128)(2,1)} %bitcast.343), channel_id=1, source_target_pairs={{0,2},{2,0},{1,3},{3,1},{4,6},{6,4},{5,7},{7,5},{8,10},{10,8},{9,1... | collective-permute-start | bytes 2654216 | tf_op jit(solution)/shard_map/ppermute | solution.py:33
  87.8 74.0 %collective-permute-start.13 = (bf16[4,24,6912]{2,1,0:T(8,128)(2,1)S(1)}, bf16[4,24,6912]{2,1,0:T(8,128)(2,1)S(1)}, u32[]{:S(2)}, u32[]{:S(2)}) collective-permute-start(bf16[4,24,6912]{2,1,0:T(8,128)(2,1)S(1)} %pad_maximum_fusion.7), channel_id=1, source_target_pairs={{0,2},{2,0},{1,3},{3,1},{4,6},{6,4},{5,7},{7,5},{8,10},{10,8},{9,1... | collective-permute-start | bytes 3981320 | tf_op jit(solution)/shard_map/ppermute | solution.py:33
  92.6 68.1 %collective-permute-start.6 = (bf16[8,24,2432]{2,1,0:T(8,128)(2,1)S(1)}, bf16[8,24,2432]{2,1,0:T(8,128)(2,1)S(1)}, u32[]{:S(2)}, u32[]{:S(2)}) collective-permute-start(bf16[8,24,2432]{2,1,0:T(8,128)(2,1)S(1)} %get-tuple-element.117), channel_id=1, source_target_pairs={{0,2},{2,0},{1,3},{3,1},{4,6},{6,4},{5,7},{7,5},{8,10},{10,8},{9,1... | collective-permute-start | bytes 2801672 | tf_op jit(solution)/shard_map/ppermute | solution.py:33
  118.7 55.5 %collective-permute-start.17 = (bf16[2,2,12,12,768]{4,1,3,2,0:T(2,128)(2,1)S(1)}, bf16[2,2,12,12,768]{4,1,3,2,0:T(2,128)(2,1)S(1)}, u32[]{:S(2)}, u32[]{:S(2)}) collective-permute-start(bf16[2,2,12,12,768]{4,1,3,2,0:T(2,128)(2,1)S(1)} %get-tuple-element.99), channel_id=1, source_target_pairs={{0,1},{1,0},{2,3},{3,2},{4,5},{5,4},{6,7},{7,6},{8,9},{9,8},{10,11... | collective-permute-start | bytes 2654216 | tf_op jit(solution)/shard_map/ppermute | solution.py:33
  120.0 44.5 %collective-permute-start.1 = (bf16[2,2,12,12,768]{4,1,3,2,0:T(2,128)(2,1)S(1)}, bf16[2,2,12,12,768]{4,1,3,2,0:T(2,128)(2,1)S(1)}, u32[]{:S(2)}, u32[]{:S(2)}) collective-permute-start(bf16[2,2,12,12,768]{4,1,3,2,0:T(2,128)(2,1)S(1)} %get-tuple-element.103), channel_id=1, source_target_pairs={{0,1},{1,0},{2,3},{3,2},{4,5},{5,4},{6,7},{7,6},{8,9},{9,8},{10,11... | collective-permute-start | bytes 2654216 | tf_op jit(solution)/shard_map/ppermute | solution.py:33
  161.8 101.5 %collective-permute-start.7 = (bf16[16,24,2432]{2,1,0:T(8,128)(2,1)}, bf16[16,24,2432]{2,1,0:T(8,128)(2,1)}, u32[]{:S(2)}, u32[]{:S(2)}) collective-permute-start(bf16[16,24,2432]{2,1,0:T(8,128)(2,1)} %constant_dynamic-update-slice_fusion.5.mine_ref), channel_id=1, source_target_pairs={{0,1},{1,0},{2,3},{3,2},{4,5},{5,4},{6,7},{7,6},{8,9},{9,8},{10,11... | collective-permute-start | bytes 5603336 | tf_op jit(solution)/shard_map/ppermute | solution.py:33
  163.0 60.0 %collective-permute-start.14 = (bf16[8,24,6912]{2,1,0:T(8,128)(2,1)S(1)}, bf16[8,24,6912]{2,1,0:T(8,128)(2,1)S(1)}, u32[]{:S(2)}, u32[]{:S(2)}) collective-permute-start(bf16[8,24,6912]{2,1,0:T(8,128)(2,1)S(1)} %get-tuple-element.106), channel_id=1, source_target_pairs={{0,4},{4,0},{8,12},{12,8},{16,20},{20,16},{24,28},{28,24},{1,5},{5... | collective-permute-start | bytes 7962632 | tf_op jit(solution)/shard_map/ppermute | solution.py:33
  224.7 125.1 %collective-permute-start.15 = (bf16[16,24,6912]{2,1,0:T(8,128)(2,1)}, bf16[16,24,6912]{2,1,0:T(8,128)(2,1)}, u32[]{:S(2)}, u32[]{:S(2)}) collective-permute-start(bf16[16,24,6912]{2,1,0:T(8,128)(2,1)} %constant_dynamic-update-slice_fusion.22.mine_ref), channel_id=1, source_target_pairs={{0,1},{1,0},{2,3},{3,2},{4,5},{5,4},{6,7},{7,6},{8,9},{9,8},{10,11... | collective-permute-start | bytes 15925256 | tf_op jit(solution)/shard_map/ppermute | solution.py:33
  533.1 49.1 %collective-permute-start.33 = (bf16[16,24,768]{2,1,0:T(8,128)(2,1)}, bf16[16,24,768]{2,1,0:T(8,128)(2,1)}, u32[]{:S(2)}, u32[]{:S(2)}) collective-permute-start(bf16[16,24,768]{2,1,0:T(8,128)(2,1)} %dynamic-slice_bitcast_fusion.15), channel_id=1, source_target_pairs={{0,1},{1,0},{2,3},{3,2},{4,5},{5,4},{6,7},{7,6},{8,9},{9,8},{10,11... | collective-permute-start | bytes 1769480 | tf_op jit(solution)/shard_map/ppermute | solution.py:33
  533.6 67.8 %collective-permute-start.20 = (bf16[2,2,12,12,768]{4,1,3,2,0:T(2,128)(2,1)}, bf16[2,2,12,12,768]{4,1,3,2,0:T(2,128)(2,1)}, u32[]{:S(2)}, u32[]{:S(2)}) collective-permute-start(bf16[2,2,12,12,768]{4,1,3,2,0:T(2,128)(2,1)} %get-tuple-element.93), channel_id=1, source_target_pairs={{0,1},{1,0},{2,3},{3,2},{4,5},{5,4},{6,7},{7,6},{8,9},{9,8},{10,11... | collective-permute-start | bytes 2654216 | tf_op jit(solution)/shard_map/ppermute | solution.py:33
  565.0 57.6 %collective-permute-start.22 = (bf16[16,24,2304]{2,1,0:T(8,128)(2,1)}, bf16[16,24,2304]{2,1,0:T(8,128)(2,1)}, u32[]{:S(2)}, u32[]{:S(2)}) collective-permute-start(bf16[16,24,2304]{2,1,0:T(8,128)(2,1)} %dynamic-slice_bitcast_fusion.2), channel_id=1, source_target_pairs={{0,1},{1,0},{2,3},{3,2},{4,5},{5,4},{6,7},{7,6},{8,9},{9,8},{10,11... | collective-permute-start | bytes 5308424 | tf_op jit(solution)/shard_map/ppermute | solution.py:33
  570.5 35.6 %collective-permute-start.18 = (bf16[2,2,12,12,768]{4,1,3,2,0:T(2,128)(2,1)}, bf16[2,2,12,12,768]{4,1,3,2,0:T(2,128)(2,1)}, u32[]{:S(2)}, u32[]{:S(2)}) collective-permute-start(bf16[2,2,12,12,768]{4,1,3,2,0:T(2,128)(2,1)} %get-tuple-element.97), channel_id=1, source_target_pairs={{0,1},{1,0},{2,3},{3,2},{4,5},{5,4},{6,7},{7,6},{8,9},{9,8},{10,11... | collective-permute-start | bytes 2654216 | tf_op jit(solution)/shard_map/ppermute | solution.py:33
  582.1 97.4 %collective-permute-start.45 = (bf16[16,96,768]{2,1,0:T(8,128)(2,1)}, bf16[16,96,768]{2,1,0:T(8,128)(2,1)}, u32[]{:S(2)}, u32[]{:S(2)}) collective-permute-start(bf16[16,96,768]{2,1,0:T(8,128)(2,1)} %dynamic-slice_bitcast_fusion), channel_id=1, source_target_pairs={{0,1},{1,0},{2,3},{3,2},{4,5},{5,4},{6,7},{7,6},{8,9},{9,8},{10,11... | collective-permute-start | bytes 7077896 | tf_op jit(solution)/shard_map/ppermute | solution.py:33
  618.1 68.1 %collective-permute-start.39 = (bf16[16,24,3072]{2,1,0:T(8,128)(2,1)}, bf16[16,24,3072]{2,1,0:T(8,128)(2,1)}, u32[]{:S(2)}, u32[]{:S(2)}) collective-permute-start(bf16[16,24,3072]{2,1,0:T(8,128)(2,1)} %dynamic-slice_bitcast_fusion.1), channel_id=1, source_target_pairs={{0,1},{1,0},{2,3},{3,2},{4,5},{5,4},{6,7},{7,6},{8,9},{9,8},{10,11... | collective-permute-start | bytes 7077896 | tf_op jit(solution)/shard_map/ppermute | solution.py:33
  621.2 38.0 %collective-permute-start.19 = (bf16[2,2,12,12,768]{4,1,3,2,0:T(2,128)(2,1)S(1)}, bf16[2,2,12,12,768]{4,1,3,2,0:T(2,128)(2,1)S(1)}, u32[]{:S(2)}, u32[]{:S(2)}) collective-permute-start(bf16[2,2,12,12,768]{4,1,3,2,0:T(2,128)(2,1)S(1)} %get-tuple-element.95), channel_id=1, source_target_pairs={{0,2},{2,0},{1,3},{3,1},{4,6},{6,4},{5,7},{7,5},{8,10},{10,8},{9,1... | collective-permute-start | bytes 2654216 | tf_op jit(solution)/shard_map/ppermute | solution.py:33
  625.4 58.0 %collective-permute-start.23 = (bf16[2,4,24,2304]{3,2,0,1:T(8,128)(2,1)}, bf16[2,4,24,2304]{3,2,0,1:T(8,128)(2,1)}, u32[]{:S(2)}, u32[]{:S(2)}) collective-permute-start(bf16[2,4,24,2304]{3,2,0,1:T(8,128)(2,1)} %fusion.28), channel_id=1, source_target_pairs={{0,4},{4,0},{8,12},{12,8},{16,20},{20,16},{24,28},{28,24},{1,5},{5... | collective-permute-start | bytes 2654216 | tf_op jit(solution)/shard_map/ppermute | solution.py:33
  682.7 41.0 %collective-permute-start.46 = (bf16[2,4,96,768]{3,2,0,1:T(8,128)(2,1)S(1)}, bf16[2,4,96,768]{3,2,0,1:T(8,128)(2,1)S(1)}, u32[]{:S(2)}, u32[]{:S(2)}) collective-permute-start(bf16[2,4,96,768]{3,2,0,1:T(8,128)(2,1)S(1)} %fusion.27), channel_id=1, source_target_pairs={{0,2},{2,0},{1,3},{3,1},{4,6},{6,4},{5,7},{7,5},{8,10},{10,8},{9,1... | collective-permute-start | bytes 3538952 | tf_op jit(solution)/shard_map/ppermute | solution.py:33
  684.8 33.5 %collective-permute-start.24 = (bf16[4,24,2304]{2,1,0:T(8,128)(2,1)S(1)}, bf16[4,24,2304]{2,1,0:T(8,128)(2,1)S(1)}, u32[]{:S(2)}, u32[]{:S(2)}) collective-permute-start(bf16[4,24,2304]{2,1,0:T(8,128)(2,1)S(1)} %fusion.31), channel_id=1, source_target_pairs={{0,2},{2,0},{1,3},{3,1},{4,6},{6,4},{5,7},{7,5},{8,10},{10,8},{9,1... | collective-permute-start | bytes 1327112 | tf_op jit(solution)/shard_map/ppermute | solution.py:33
  689.6 35.2 %collective-permute-start.40 = (bf16[2,4,24,3072]{3,2,0,1:T(8,128)(2,1)S(1)}, bf16[2,4,24,3072]{3,2,0,1:T(8,128)(2,1)S(1)}, u32[]{:S(2)}, u32[]{:S(2)}) collective-permute-start(bf16[2,4,24,3072]{3,2,0,1:T(8,128)(2,1)S(1)} %fusion.26), channel_id=1, source_target_pairs={{0,4},{4,0},{8,12},{12,8},{16,20},{20,16},{24,28},{28,24},{1,5},{5... | collective-permute-start | bytes 3538952 | tf_op jit(solution)/shard_map/ppermute | solution.py:33
  (72 other events, 804.2 us)
